TPU v7x, 512 devices: a whole 4x8x8 slice. The times are simulated.
512 devices in a mesh: gx: 8 (over z), gy: 8 (over x, y_lo), gz: 8 (over y_hi, core).
Axes of the slice: x: 4, y: 8 (y_hi: 4, y_lo: 2; y = y_hi * 2 + y_lo), z: 8, core: 2. Of those that a mesh axis runs over, the one named last changes fastest.
Arguments:
- inputs: bfloat16 [512, 12288], P(('gx', 'gy'), 'gz'), may hold values from -6 to 6
- out_grad: bfloat16 [512, 12288], P(('gx', 'gy'), 'gz'), may hold values from -6 to 6
- preact: bfloat16 [512, 24576], P('gz', ('gx', 'gy')), may hold values from -6 to 6
- w_in: bfloat16 [12288, 24576], P('gz', ('gx', 'gy')), may hold values from -0.0546875 to 0.0546875
- w_out: bfloat16 [24576, 12288], P(('gx', 'gy'), 'gz'), may hold values from -0.0390625 to 0.0390625
Outputs:
- grad_input: bfloat16 [512, 12288], P(('gx', 'gy'), 'gz')
- grad_w_in: bfloat16 [12288, 24576], P('gz', ('gx', 'gy'))
- grad_w_out: bfloat16 [24576, 12288], P(('gx', 'gy'), 'gz')
All inputs are finite; a program needn't handle non-finite values.
Results may differ from a plain program's by a relative error of at most 0.0049.
Values may be sent and summed in bfloat16 or wider, within the bound.
No kernel may reach another device: no remote copies, remote signals or barrier semaphores. Data moves between devices by JAX's collectives and lax.ppermute only.
A program may use at most 64 MiB of HBM per device.

v0:
```python
import jax
import jax.numpy as jnp
from jax import lax
from jax.sharding import PartitionSpec as P

gelu_scale = 0.7978845608028654
cubic_coef = 0.044715


def gelu_parts(pre_float):
    tanh_arg = gelu_scale * (pre_float + cubic_coef * pre_float * pre_float * pre_float)
    tangent = jnp.tanh(tanh_arg)
    value = 0.5 * pre_float * (1.0 + tangent)
    slope = 0.5 * (1.0 + tangent) + 0.5 * pre_float * (1.0 - tangent * tangent) * gelu_scale * (
        1.0 + 3.0 * cubic_coef * pre_float * pre_float
    )
    return (value, slope)


def contract_rows(left, right):
    return lax.dot_general(
        left, right, (((1,), (1,)), ((), ())), preferred_element_type=jnp.float32
    )


def contract_cols(left, right):
    return lax.dot_general(
        left, right, (((0,), (0,)), ((), ())), preferred_element_type=jnp.float32
    )


def on_device(inputs, out_grad, preact, w_in, w_out):
    rows_x, rows_dy = (
        lax.all_gather(inputs, ("gx", "gy"), axis=0, tiled=True),
        lax.all_gather(out_grad, ("gx", "gy"), axis=0, tiled=True),
    )
    picked = rows_dy
    grad_hidden = lax.psum_scatter(
        contract_rows(picked, w_out), "gz", scatter_dimension=0, tiled=True
    )
    value_local, slope_local = gelu_parts(preact.astype(jnp.float32))
    grad_pre = (grad_hidden * slope_local).astype(jnp.bfloat16)
    hidden_local = value_local.astype(jnp.bfloat16)
    grad_all, hidden_all = (
        lax.all_gather(grad_pre, "gz", axis=0, tiled=True),
        lax.all_gather(hidden_local, "gz", axis=0, tiled=True),
    )
    grad_w_out = contract_cols(hidden_all, rows_dy).astype(jnp.bfloat16)
    grad_w_in = contract_cols(rows_x, grad_all).astype(jnp.bfloat16)
    picked = grad_all
    grad_input = lax.psum_scatter(
        contract_rows(picked, w_in), ("gx", "gy"), scatter_dimension=0, tiled=True
    ).astype(jnp.bfloat16)
    return (grad_input, grad_w_in, grad_w_out)


def solution(mesh):
    in_specs = (
        P(("gx", "gy"), "gz"),
        P(("gx", "gy"), "gz"),
        P("gz", ("gx", "gy")),
        P("gz", ("gx", "gy")),
        P(("gx", "gy"), "gz"),
    )
    out_specs = (P(("gx", "gy"), "gz"), P("gz", ("gx", "gy")), P(("gx", "gy"), "gz"))
    return jax.shard_map(
        on_device, mesh=mesh, in_specs=in_specs, out_specs=out_specs, check_vma=False
    )
```

profile of v0, /device:TPU:16, one launch (start us, length us, event | category | flops | bytes accessed | tf_op | source)
XLA Modules:
  0.0 995.1 jit_solution(596862571673999329)
XLA Ops:
  7.2 0.0 copy-start
  7.2 0.0 all-gather.3.cloned.1.call-start
  7.2 0.7 all-gather.3.cloned.1.call-update
  7.9 0.0 copy-start.1
  7.9 0.0 reduce-scatter.3.cloned.1.call-start
  8.0 309.0 %all-gather.3.cloned.1.call-done = bf16[512,1536]{1,0:T(8,128)(2,1)} async-done(((bf16[8,1536]{1,0:T(8,128)(2,1)}), bf16[512,1536]{1,0:T(8,128)(2,1)}) %all-gather.3.cloned.1.call-update) | async-done | bytes 1572880 | tf_op jit(solution)/shard_map/all_gather | solution.py:35
  317.0 3.6 fusion.12
  320.6 0.0 reduce-scatter.3.cloned.1.call-update
  320.6 0.0 all-gather.5.cloned.1.call-start
  320.7 0.7 all-gather.5.cloned.1.call-update
  321.4 0.0 reduce-scatter.5.cloned.1.call-start
  321.4 32.7 %reduce-scatter.3.cloned.1.call-done = f32[64,384]{1,0:T(8,128)} async-done(((f32[512,384]{1,0:T(8,128)}), f32[64,384]{1,0:T(8,128)}) %reduce-scatter.3.cloned.1.call-update) | async-done | bytes 98320 | tf_op jit(solution)/shard_map/reduce_scatter | solution.py:38
  354.1 0.0 copy-done.1
  354.1 1.0 fusion.8
  355.1 16.7 %all_gather.13 = bf16[512,384]{1,0:T(8,128)(2,1)S(1)} all-gather(bf16[64,384]{1,0:T(8,128)(2,1)S(1)} %get-tuple-element.7), channel_id=1, replica_groups=mesh['gx'=8,'gy'=8,'gz'=8] {'gz'}, dimensions={0}, use_global_device_ids=true | all-gather | bytes 442368 | tf_op jit(solution)/shard_map/all_gather | solution.py:45
  371.7 0.0 copy-done
  371.8 2.6 fusion.13
  374.4 0.0 reduce-scatter.5.cloned.1.call-update
  374.4 287.2 %all-gather.5.cloned.1.call-done = bf16[512,1536]{1,0:T(8,128)(2,1)} async-done(((bf16[8,1536]{1,0:T(8,128)(2,1)}), bf16[512,1536]{1,0:T(8,128)(2,1)}) %all-gather.5.cloned.1.call-update) | async-done | bytes 1572880 | tf_op jit(solution)/shard_map/all_gather | solution.py:34
  661.6 2.2 fusion
  663.8 1.4 copy.8
  665.2 15.2 %all_gather.15 = bf16[512,384]{1,0:T(8,128)(2,1)S(1)} all-gather(bf16[64,384]{1,0:T(8,128)(2,1)S(1)} %get-tuple-element.6), channel_id=1, replica_groups=mesh['gx'=8,'gy'=8,'gz'=8] {'gz'}, dimensions={0}, use_global_device_ids=true | all-gather | bytes 442368 | tf_op jit(solution)/shard_map/all_gather | solution.py:46
  680.4 3.2 convolution_convert_fusion
  683.6 303.5 %reduce-scatter.5.cloned.1.call-done = f32[8,1536]{1,0:T(8,128)} async-done(((f32[512,1536]{1,0:T(8,128)}), f32[8,1536]{1,0:T(8,128)}) %reduce-scatter.5.cloned.1.call-update) | async-done | bytes 49168 | tf_op jit(solution)/shard_map/reduce_scatter | solution.py:51
  987.2 1.4 convert_element_type.23
Async XLA Ops:
  7.2 364.6 %copy-start = (bf16[1536,384]{1,0:T(8,128)(2,1)S(1)}, bf16[1536,384]{1,0:T(8,128)(2,1)}, u32[]{:S(2)}) copy-start(bf16[1536,384]{1,0:T(8,128)(2,1)} %param.8) | copy-start | bytes 3538948
  7.2 309.8 %all-gather.3.cloned.1.call-start = ((), (), s32[]{:S(2)}) async-start(), calls=%async_computation.2 | async-start | bytes 1597440 | tf_op jit(solution)/shard_map/all_gather | solution.py:35
  7.9 346.2 %copy-start.1 = (bf16[64,384]{1,0:T(8,128)(2,1)S(1)}, bf16[64,384]{1,0:T(8,128)(2,1)}, u32[]{:S(2)}) copy-start(bf16[64,384]{1,0:T(8,128)(2,1)} %param.7) | copy-start | bytes 147460
  7.9 346.2 %reduce-scatter.3.cloned.1.call-start = ((), (), s32[]{:S(2)}) async-start(), calls=%async_computation.3 | async-start | bytes 884736 | tf_op jit(solution)/shard_map/reduce_scatter | solution.py:38
  320.6 341.0 %all-gather.5.cloned.1.call-start = ((), (), s32[]{:S(2)}) async-start(), calls=%async_computation.5 | async-start | bytes 1597440 | tf_op jit(solution)/shard_map/all_gather | solution.py:34
  321.4 665.8 %reduce-scatter.5.cloned.1.call-start = ((), (), s32[]{:S(2)}) async-start(), calls=%async_computation.4 | async-start | bytes 3194880 | tf_op jit(solution)/shard_map/reduce_scatter | solution.py:51
Sparse Core Ops, SparseCore 0:
  10.1 306.8 all-gather.2
  320.8 33.3 reduce-scatter.2
  356.4 305.1 all-gather.4
  664.5 322.6 reduce-scatter.4
where the time goes:
time: 995 us
  waiting for transfers between devices  934 us (94%)
  blocking collectives  31.8 us (3%)
  between operations  13.8 us (1%)
  matrix products  11.7 us (1%)
    all_gather x1, waiting for transfers between devices, on_device(): lax.all_gather(out_grad, ('gx', 'gy'), axis=0, tiled=True)  309 us
    reduce_scatter x1, waiting for transfers between devices, on_device(): lax.psum_scatter(contract_rows(picked, w_in), ('gx', 'gy'), scatter_dimen...  304 us
    all_gather x1, waiting for transfers between devices, on_device(): lax.all_gather(inputs, ('gx', 'gy'), axis=0, tiled=True)  287 us
    reduce_scatter x1, waiting for transfers between devices, on_device(): lax.psum_scatter(contract_rows(picked, w_out), 'gz', scatter_dimension=0,...  32.7 us
  transfers between devices with their start and end apart: 4, of which 4 were waited for; matrix products, arithmetic and copies ran while one was open for 1% of the time, Pallas kernels for 0%

commit v1 on v0

--- a/solution.py
+++ b/solution.py
@@ -1,3 +1,4 @@
+import functools
 import jax
 import jax.numpy as jnp
 from jax import lax
@@ -5,6 +6,15 @@
 
 gelu_scale = 0.7978845608028654
 cubic_coef = 0.044715
+
+
+def connect_patch_on(page, group_axis):
+    return jnp.concatenate(
+        lax.all_to_all(jnp.stack([page] * lax.psum(1, group_axis)), group_axis, 0, 0), axis=0
+    )
+
+
+enter_sizes = functools.partial(connect_patch_on, group_axis=("gx", "gy"))
 
 
 def gelu_parts(pre_float):
@@ -31,7 +41,7 @@
 
 def on_device(inputs, out_grad, preact, w_in, w_out):
     rows_x, rows_dy = (
-        lax.all_gather(inputs, ("gx", "gy"), axis=0, tiled=True),
+        enter_sizes(inputs),
         lax.all_gather(out_grad, ("gx", "gy"), axis=0, tiled=True),
     )
     picked = rows_dy

time: 995 us -> 712 us (0.72)
  waiting for transfers between devices: 934 us -> 598 us
  blocking collectives: 31.8 us -> 85.4 us
    all_gather x1 -> x0, waiting for transfers between devices: 287 us -> none  [on_device(): lax.all_gather(inputs, ('gx', 'gy'), axis=0, tiled=True)]
    all_to_all x0 -> x1, blocking collectives: none -> 53.5 us  [connect_patch_on(): lax.all_to_all(jnp.stack([page] * lax.psum(1, group_axis)), group_axis, 0...]
    reduce_scatter x1, waiting for transfers between devices: 304 us -> 255 us  [on_device(): lax.psum_scatter(contract_rows(picked, w_in), ('gx', 'gy'), scatter_dimen...]
  transfers between devices with their start and end apart: 4 -> 3, of which waited for: 4 -> 3; matrix products, arithmetic and copies ran while one was open for 1% -> 1% of each run, Pallas kernels for 0% -> 0%
where the time goes in v1:
time: 712 us
  waiting for transfers between devices  598 us (84%)
  blocking collectives  85.4 us (12%)
  between operations  13.8 us (2%)
  matrix products  10.3 us (1%)
    all_gather x1, waiting for transfers between devices, on_device(): lax.all_gather(out_grad, ('gx', 'gy'), axis=0, tiled=True)  309 us
    reduce_scatter x1, waiting for transfers between devices, on_device(): lax.psum_scatter(contract_rows(picked, w_in), ('gx', 'gy'), scatter_dimen...  255 us
    all_to_all x1, blocking collectives, connect_patch_on(): lax.all_to_all(jnp.stack([page] * lax.psum(1, group_axis)), group_axis, 0...  53.5 us
    reduce_scatter x1, waiting for transfers between devices, on_device(): lax.psum_scatter(contract_rows(picked, w_out), 'gz', scatter_dimension=0,...  33.4 us
    all_gather x1, blocking collectives, on_device(): lax.all_gather(grad_pre, 'gz', axis=0, tiled=True)  16.7 us
    all_gather x1, blocking collectives, on_device(): lax.all_gather(hidden_local, 'gz', axis=0, tiled=True)  15.3 us
  transfers between devices with their start and end apart: 3, of which 3 were waited for; matrix products, arithmetic and copies ran while one was open for 1% of the time, Pallas kernels for 0%

profile of v1, /device:TPU:16, one launch (start us, length us, event | category | flops | bytes accessed | tf_op | source)
XLA Modules:
  0.0 712.1 jit_solution(5221708911343416166)
XLA Ops:
  7.2 0.0 copy-start
  7.2 0.0 all-gather.2.cloned.1.call-start
  7.2 0.7 all-gather.2.cloned.1.call-update
  7.9 0.0 copy-start.1
  7.9 0.0 reduce-scatter.3.cloned.1.call-start
  8.0 309.0 %all-gather.2.cloned.1.call-done = bf16[512,1536]{1,0:T(8,128)(2,1)} async-done(((bf16[8,1536]{1,0:T(8,128)(2,1)}), bf16[512,1536]{1,0:T(8,128)(2,1)}) %all-gather.2.cloned.1.call-update) | async-done | bytes 1572880 | tf_op jit(solution)/shard_map/all_gather | solution.py:45
  317.0 3.6 fusion.13
  320.6 0.0 reduce-scatter.3.cloned.1.call-update
  320.6 0.0 reduce-scatter.5.cloned.1.call-start
  320.7 33.4 %reduce-scatter.3.cloned.1.call-done = f32[64,384]{1,0:T(8,128)} async-done(((f32[512,384]{1,0:T(8,128)}), f32[64,384]{1,0:T(8,128)}) %reduce-scatter.3.cloned.1.call-update) | async-done | bytes 98320 | tf_op jit(solution)/shard_map/reduce_scatter | solution.py:48
  354.1 0.0 copy-done.1
  354.1 1.0 fusion.9
  355.1 16.7 %all_gather.10 = bf16[512,384]{1,0:T(8,128)(2,1)S(1)} all-gather(bf16[64,384]{1,0:T(8,128)(2,1)S(1)} %get-tuple-element.7), channel_id=1, replica_groups=mesh['gx'=8,'gy'=8,'gz'=8] {'gz'}, dimensions={0}, use_global_device_ids=true | all-gather | bytes 442368 | tf_op jit(solution)/shard_map/all_gather | solution.py:55
  371.7 0.0 copy-done
  371.8 2.7 fusion.14
  374.4 0.0 copy-start.2
  374.4 0.0 reduce-scatter.5.cloned.1.call-update
  374.4 0.7 copy-done.2
  375.1 0.1 stack.2
  375.3 53.5 %all_to_all.5 = bf16[64,8,1536]{2,1,0:T(8,128)(2,1)S(1)} all-to-all(bf16[64,8,1536]{2,1,0:T(8,128)(2,1)S(1)} %stack.2), channel_id=1, replica_groups=mesh['gx'=8,'gy'=8,'gz'=8] {'gx','gy'}, dimensions={0} | all-to-all | bytes 3145728 | tf_op jit(solution)/shard_map/all_to_all | solution.py:13
  428.7 0.8 fusion
  429.5 1.4 copy.8
  430.9 15.3 %all_gather.11 = bf16[512,384]{1,0:T(8,128)(2,1)S(1)} all-gather(bf16[64,384]{1,0:T(8,128)(2,1)S(1)} %get-tuple-element.6), channel_id=1, replica_groups=mesh['gx'=8,'gy'=8,'gz'=8] {'gz'}, dimensions={0}, use_global_device_ids=true | all-gather | bytes 442368 | tf_op jit(solution)/shard_map/all_gather | solution.py:56
  446.2 3.2 convolution_convert_fusion
  449.4 254.7 %reduce-scatter.5.cloned.1.call-done = f32[8,1536]{1,0:T(8,128)} async-done(((f32[512,1536]{1,0:T(8,128)}), f32[8,1536]{1,0:T(8,128)}) %reduce-scatter.5.cloned.1.call-update) | async-done | bytes 49168 | tf_op jit(solution)/shard_map/reduce_scatter | solution.py:61
  704.2 1.4 convert_element_type.23
Async XLA Ops:
  7.2 364.6 %copy-start = (bf16[1536,384]{1,0:T(8,128)(2,1)S(1)}, bf16[1536,384]{1,0:T(8,128)(2,1)}, u32[]{:S(2)}) copy-start(bf16[1536,384]{1,0:T(8,128)(2,1)} %param.8) | copy-start | bytes 3538948
  7.2 309.8 %all-gather.2.cloned.1.call-start = ((), (), s32[]{:S(2)}) async-start(), calls=%async_computation.3 | async-start | bytes 1597440 | tf_op jit(solution)/shard_map/all_gather | solution.py:45
  7.9 346.2 %copy-start.1 = (bf16[64,384]{1,0:T(8,128)(2,1)S(1)}, bf16[64,384]{1,0:T(8,128)(2,1)}, u32[]{:S(2)}) copy-start(bf16[64,384]{1,0:T(8,128)(2,1)} %param.7) | copy-start | bytes 147460
  7.9 346.2 %reduce-scatter.3.cloned.1.call-start = ((), (), s32[]{:S(2)}) async-start(), calls=%async_computation.4 | async-start | bytes 884736 | tf_op jit(solution)/shard_map/reduce_scatter | solution.py:48
  320.6 383.5 %reduce-scatter.5.cloned.1.call-start = ((), (), s32[]{:S(2)}) async-start(), calls=%async_computation.5 | async-start | bytes 3194880 | tf_op jit(solution)/shard_map/reduce_scatter | solution.py:61
  374.4 0.7 copy-start.2
Sparse Core Ops, SparseCore 0:
  10.1 306.8 all-gather.1
  320.8 33.3 reduce-scatter.2
  374.6 329.5 reduce-scatter.4
